TPU v7x, 512 devices: a whole 4x8x8 slice. The times are simulated.
512 devices in a mesh: blk: 16 (over z_lo, x), lab: 32 (over y, z_hi, core).
Axes of the slice: x: 4, y: 8, z: 8 (z_hi: 2, z_lo: 4; z = z_hi * 4 + z_lo), core: 2. Of those that a mesh axis runs over, the one named last changes fastest.
Arguments:
- features: bfloat16 [65536, 768], P(('blk', 'lab')), may hold values from -0.21875 to 0.21875
- direction: bfloat16 [32, 256, 768], P('lab', 'blk'), may hold values from -6 to 6
- active: int32 [65536, 8192], P('blk', 'lab'), may hold values 0 or 1
- shortlist: int32 [512, 64], P('blk', 'lab'), may hold values 0 or 1
Outputs:
- hess_product: float32 [32, 256, 768], P('lab', 'blk')
- curvature: float32 [32, 256], P('lab', 'blk')
All inputs are finite; a program needn't handle non-finite values. No bound on the sum of `active` or of `shortlist` on one device may be relied on, other than what follows from the above.
Results may differ from a plain program's by a relative error of at most 0.00059.
Values may be sent and summed in bfloat16 or wider, within the bound.
No kernel may reach another device: no remote copies, remote signals or barrier semaphores. Data moves between devices by JAX's collectives and lax.ppermute only.
A program may use at most 64 MiB of HBM per device.

v0:
```python
import jax
import jax.numpy as jnp
from jax import lax
from jax.sharding import PartitionSpec as P

D = 768
TILE = 128


def active_weights(active, shortlist):
    row_tiles, label_tiles = shortlist.shape
    blocks = active.reshape(row_tiles, TILE, label_tiles, TILE) * shortlist[:, None, :, None]
    return blocks.reshape(active.shape).astype(jnp.bfloat16)


def shards(features, direction, active, shortlist):
    vectors = direction[0]
    gathered = lax.all_gather(vectors, "blk", axis=0, tiled=True)
    weights = active_weights(active, shortlist)
    slab_part = lax.all_gather(features, "lab", axis=0, tiled=True)
    margins = lax.dot_general(
        slab_part, gathered, (((1,), (1,)), ((), ())), preferred_element_type=jnp.float32
    )
    scaled = (weights.astype(jnp.float32) * margins).astype(jnp.bfloat16)
    label_sums = lax.dot_general(
        scaled, slab_part, (((0,), (0,)), ((), ())), preferred_element_type=jnp.float32
    )
    own_total = lax.psum_scatter(label_sums, "blk", scatter_dimension=0, tiled=True)
    product = vectors.astype(jnp.float32) + own_total
    curve = jnp.sum(vectors.astype(jnp.float32) * product, axis=-1) / D
    return (product[None], curve[None])


def solution(mesh):
    return jax.shard_map(
        shards,
        mesh=mesh,
        in_specs=(P(("blk", "lab"), None), P("lab", "blk", None), P("blk", "lab"), P("blk", "lab")),
        out_specs=(P("lab", "blk", None), P("lab", "blk")),
        check_vma=False,
    )
```

profile of v0, /device:TPU:8, one launch (start us, length us, event | category | flops | bytes accessed | tf_op | source)
XLA Modules:
  0.0 245.1 jit_solution(11948266229189764883)
XLA Ops:
  7.2 0.0 all-gather.3.cloned.1.call-start
  7.2 0.7 all-gather.3.cloned.1.call-update
  7.9 0.0 reduce-scatter.2.cloned.1.call-start
  7.9 0.8 copy.6
  8.7 47.3 %all-gather = bf16[1,256,768]{2,1,0:T(8,128)(2,1)S(1)} all-gather(bf16[1,16,768]{2,1,0:T(8,128)(2,1)} %param.5), channel_id=2, replica_groups=mesh['blk'=16,'lab'=32] {'blk'}, dimensions={1}, use_global_device_ids=true | all-gather | bytes 417792 | tf_op jit(solution)/shard_map/all_gather | solution.py:18
  56.0 79.5 %all-gather.3.cloned.1.call-done = bf16[4096,768]{1,0:T(8,128)(2,1)} async-done(((bf16[128,768]{1,0:T(8,128)(2,1)}), bf16[4096,768]{1,0:T(8,128)(2,1)}) %all-gather.3.cloned.1.call-update) | async-done | bytes 6291472 | tf_op jit(solution)/shard_map/all_gather | solution.py:20
  135.5 3.2 %mul.17 = s32[32,128,2,128]{3,2,1,0:T(2,128)} broadcast(s32[32,2]{1,0:T(8,128)S(1)} %copy.6), dimensions={0,2} | broadcast | bytes 4194560 | tf_op jit(solution)/shard_map/mul | solution.py:12
  138.7 0.0 copy-start
  138.7 13.8 %fusion.4 = f32[256,768]{1,0:T(8,128)} fusion(bf16[4096,768]{1,0:T(8,128)(2,1)} %all-gather.3.cloned.1.call-done, s32[4096,256]{1,0:T(8,128)} %param.6, s32[512,8,2,128]{3,2,1,0:T(2,128)} %bitcast.25, bf16[1,256,768]{2,1,0:T(8,128)(2,1)S(1)} %all-gather), kind=kOutput, calls=%fused_computation.5 | convolution fusion | flops 3226468352 | bytes 15859712 | tf_op jit(solution)/shard_map/dot_general | solution.py:25
  152.5 0.0 reduce-scatter.2.cloned.1.call-update
  152.5 83.7 %reduce-scatter.2.cloned.1.call-done = f32[16,768]{1,0:T(8,128)} async-done(((f32[256,768]{1,0:T(8,128)}), f32[16,768]{1,0:T(8,128)}) %reduce-scatter.2.cloned.1.call-update) | async-done | bytes 49168 | tf_op jit(solution)/shard_map/reduce_scatter | solution.py:28
  236.2 0.0 copy-done
  236.2 1.5 fusion.6
  237.7 0.5 multiply_bitcast_fusion
Async XLA Ops:
  7.2 128.4 %all-gather.3.cloned.1.call-start = ((), (), s32[]{:S(2)}) async-start(), calls=%async_computation.1 | async-start | bytes 6488064 | tf_op jit(solution)/shard_map/all_gather | solution.py:20
  7.9 228.3 %reduce-scatter.2.cloned.1.call-start = ((), (), s32[]{:S(2)}) async-start(), calls=%async_computation.2 | async-start | bytes 835584 | tf_op jit(solution)/shard_map/reduce_scatter | solution.py:28
  138.7 97.5 %copy-start = (bf16[1,16,768]{2,1,0:T(8,128)(2,1)S(1)}, bf16[1,16,768]{2,1,0:T(8,128)(2,1)}, u32[]{:S(2)}) copy-start(bf16[1,16,768]{2,1,0:T(8,128)(2,1)} %param.5) | copy-start | bytes 73732
Sparse Core Ops, SparseCore 0:
  11.3 124.2 all-gather.2
  152.6 83.4 reduce-scatter.1
where the time goes:
time: 245 us
  waiting for transfers between devices  164 us (67%)
  blocking collectives  47.3 us (19%)
  between operations  14 us (6%)
  matrix products  13.8 us (6%)
  local copies, waits for them, and re-layouts  3.93 us (2%)
    reduce_scatter x1, waiting for transfers between devices, shards(): lax.psum_scatter(label_sums, 'blk', scatter_dimension=0, tiled=True)  83.7 us
    all_gather x1, waiting for transfers between devices, shards(): slab_part = lax.all_gather(features, 'lab', axis=0, tiled=True)  79.5 us
    all_gather x1, blocking collectives, shards(): gathered = lax.all_gather(vectors, 'blk', axis=0, tiled=True)  47.3 us
    dot_general x1, matrix products, shards(): lax.dot_general(scaled, slab_part, (((0,), (0,)), ((), ())), preferred_el...  13.8 us
  transfers between devices with their start and end apart: 2, of which 2 were waited for; matrix products, arithmetic and copies ran while one was open for 0% of the time, Pallas kernels for 0%

commit v1 on v0

--- a/solution.py
+++ b/solution.py
@@ -17,7 +17,9 @@
     vectors = direction[0]
     gathered = lax.all_gather(vectors, "blk", axis=0, tiled=True)
     weights = active_weights(active, shortlist)
-    slab_part = lax.all_gather(features, "lab", axis=0, tiled=True)
+    slab_part = jnp.concatenate(
+        lax.all_to_all(jnp.stack([features] * lax.axis_size("lab")), "lab", 0, 0), axis=0
+    )
     margins = lax.dot_general(
         slab_part, gathered, (((1,), (1,)), ((), ())), preferred_element_type=jnp.float32
     )

time: 245 us -> 328 us (1.34)
  blocking collectives: 47.3 us -> 184 us
  waiting for transfers between devices: 164 us -> 89.9 us
  starting transfers between devices: 0.08 us -> 16.4 us
  local copies, waits for them, and re-layouts: 3.93 us -> 7.56 us
    all_gather x1, blocking collectives: 47.3 us -> 184 us  [shards(): gathered = lax.all_gather(vectors, 'blk', axis=0, tiled=True)]
    all_gather x1 -> x0, waiting for transfers between devices: 79.5 us -> none  [shards(): slab_part = lax.all_gather(features, 'lab', axis=0, tiled=True)]
    all_to_all x0 -> x1, starting transfers between devices: none -> 16.3 us  [shards(): lax.all_to_all(jnp.stack([features] * lax.axis_size('lab')), 'lab', 0, 0)]
    reduce_scatter x1, waiting for transfers between devices: 83.7 us -> 89.9 us  [shards(): lax.psum_scatter(label_sums, 'blk', scatter_dimension=0, tiled=True)]
    another operation x0 -> x1, local copies, waits for them, and re-layouts: none -> 4.3 us  [shards(): jnp.stack([features] * lax.axis_size('lab'))]
  transfers between devices with their start and end apart: 2 -> 2, of which waited for: 2 -> 1; matrix products, arithmetic and copies ran while one was open for 0% -> 0% of each run, Pallas kernels for 0% -> 0%
where the time goes in v1:
time: 328 us; the launch traced here: 327 us
  blocking collectives  184 us (56%)
  waiting for transfers between devices  89.9 us (27%)
  starting transfers between devices  16.4 us (5%)
  between operations  14 us (4%)
  matrix products  13.8 us (4%)
  local copies, waits for them, and re-layouts  7.56 us (2%)
    all_gather x1, blocking collectives, shards(): gathered = lax.all_gather(vectors, 'blk', axis=0, tiled=True)  184 us
    reduce_scatter x1, waiting for transfers between devices, shards(): lax.psum_scatter(label_sums, 'blk', scatter_dimension=0, tiled=True)  89.9 us
    all_to_all x1, starting transfers between devices, shards(): lax.all_to_all(jnp.stack([features] * lax.axis_size('lab')), 'lab', 0, 0)  16.3 us
    dot_general x1, matrix products, shards(): lax.dot_general(scaled, slab_part, (((0,), (0,)), ((), ())), preferred_el...  13.8 us
  transfers between devices with their start and end apart: 2, of which 1 were waited for; matrix products, arithmetic and copies ran while one was open for 0% of the time, Pallas kernels for 0%

profile of v1, /device:TPU:8, one launch (start us, length us, event | category | flops | bytes accessed | tf_op | source)
XLA Modules:
  0.0 327.4 jit_solution(12608722988592543245)
XLA Ops:
  7.2 4.3 %stack.2 = bf16[32,128,768]{2,1,0:T(8,128)(2,1)} broadcast(bf16[128,768]{1,0:T(8,128)(2,1)} %param.4), dimensions={1,2} | broadcast | bytes 6488064 | tf_op jit(solution)/shard_map/stack | solution.py:21
  11.5 0.0 copy-start.1
  11.5 0.0 copy-start
  11.5 16.3 %all-to-all-start = ((bf16[32,128,768]{2,1,0:T(8,128)(2,1)}), bf16[32,128,768]{2,1,0:T(8,128)(2,1)}, u32[]{:S(2)}, u32[]{:S(2)}) async-start(bf16[32,128,768]{2,1,0:T(8,128)(2,1)} %stack.2), calls=%async_computation | async-start | bytes 12582912 | tf_op jit(solution)/shard_map/all_to_all | solution.py:21
  27.8 0.0 reduce-scatter.2.cloned.1.call-start
  27.9 0.0 copy-done.1
  27.9 0.1 copy.6
  28.0 0.0 copy-done
  28.0 183.7 %all-gather = bf16[1,256,768]{2,1,0:T(8,128)(2,1)S(1)} all-gather(bf16[1,16,768]{2,1,0:T(8,128)(2,1)S(1)} %copy-done), channel_id=2, replica_groups=mesh['blk'=16,'lab'=32] {'blk'}, dimensions={1}, use_global_device_ids=true | all-gather | bytes 417792 | tf_op jit(solution)/shard_map/all_gather | solution.py:18
  211.6 0.0 all-to-all-done
  211.6 3.2 mul.17
  214.8 13.8 %fusion.4 = f32[256,768]{1,0:T(8,128)} fusion(bf16[4096,768]{1,0:T(8,128)(2,1)} %bitcast.1, s32[4096,256]{1,0:T(8,128)} %param.6, s32[512,8,2,128]{3,2,1,0:T(2,128)} %bitcast.26, bf16[1,256,768]{2,1,0:T(8,128)(2,1)S(1)} %all-gather), kind=kOutput, calls=%fused_computation.5 | convolution fusion | flops 3226468352 | bytes 15859712 | tf_op jit(solution)/shard_map/dot_general | solution.py:27
  228.6 0.0 reduce-scatter.2.cloned.1.call-update
  228.6 89.9 %reduce-scatter.2.cloned.1.call-done = f32[16,768]{1,0:T(8,128)} async-done(((f32[256,768]{1,0:T(8,128)}), f32[16,768]{1,0:T(8,128)}) %reduce-scatter.2.cloned.1.call-update) | async-done | bytes 49168 | tf_op jit(solution)/shard_map/reduce_scatter | solution.py:30
  318.5 1.5 fusion.6
  320.0 0.5 multiply_bitcast_fusion
Async XLA Ops:
  11.5 16.4 %copy-start.1 = (s32[32,2]{0,1:T(2,128)S(1)}, s32[32,2]{0,1:T(2,128)}, u32[]{:S(2)}) copy-start(s32[32,2]{0,1:T(2,128)} %param.7) | copy-start | bytes 772
  11.5 16.5 %copy-start = (bf16[1,16,768]{2,1,0:T(8,128)(2,1)S(1)}, bf16[1,16,768]{2,1,0:T(8,128)(2,1)}, u32[]{:S(2)}) copy-start(bf16[1,16,768]{2,1,0:T(8,128)(2,1)} %param.5) | copy-start | bytes 73732
  11.5 200.1 %all-to-all-start = ((bf16[32,128,768]{2,1,0:T(8,128)(2,1)}), bf16[32,128,768]{2,1,0:T(8,128)(2,1)}, u32[]{:S(2)}, u32[]{:S(2)}) async-start(bf16[32,128,768]{2,1,0:T(8,128)(2,1)} %stack.2), calls=%async_computation | async-start | bytes 12582912 | tf_op jit(solution)/shard_map/all_to_all | solution.py:21
  27.8 290.7 %reduce-scatter.2.cloned.1.call-start = ((), (), s32[]{:S(2)}) async-start(), calls=%async_computation.2 | async-start | bytes 835584 | tf_op jit(solution)/shard_map/reduce_scatter | solution.py:30
Sparse Core Ops, SparseCore 0:
  228.7 89.7 reduce-scatter.1
